TPU v7x, 32 devices: a whole 2x2x4 slice. The times are simulated.
32 devices in a mesh: slab: 8 (over z, core), row: 4 (over y, x).
Axes of the slice: x: 2, y: 2, z: 4, core: 2. Of those that a mesh axis runs over, the one named last changes fastest.
Arguments:
- propagator_matrices: float32 [16, 512, 512], P('slab', 'row'), may hold values from -1 to 2
- gain: float32 [512, 128], replicated, may hold values from -0.0546875 to 0.0546875
- obs_matrix: float32 [128, 512], replicated, may hold values from -0.25 to 0.25
- observations: float32 [16, 128], P('slab'), may hold values from -6 to 6
- present: int32 [16], P('slab'), may hold values 0 or 1
- initial: float32 [512], replicated, may hold values from -6 to 6
- smoother_gain: float32 [512, 512], P('row'), may hold values from -1 to 2
Outputs:
- filtered: float32 [16, 512], P('slab')
- smoothed: float32 [16, 512], P('slab')
All inputs are finite; a program needn't handle non-finite values. No bound on the sum of `present` on one device may be relied on, other than what follows from the above.
Results may differ from a plain program's by a relative error of at most 0.00015.
Values sent between devices are 32-bit elements; how exact they have to be, the bound alone decides.
No kernel may reach another device: no remote copies, remote signals or barrier semaphores. Data moves between devices by JAX's collectives and lax.ppermute only.
A program may use at most 192 MiB of HBM per device.

v0:
```python
import jax
import jax.numpy as jnp
from jax import lax
from jax.sharding import PartitionSpec as P


def carried_in(part, axis, combine, identity, reverse):
    count = lax.axis_size(axis)
    place = lax.axis_index(axis)
    ahead = count - 1 - place if reverse else place
    gathered = jax.tree.map(lambda a: lax.all_gather(a, axis), part)
    state = jax.tree.map(lambda a, e: jnp.zeros_like(a) + jnp.asarray(e, a.dtype), part, identity)

    def one(step, state):
        source = count - 1 - step if reverse else step
        return combine(
            state, jax.tree.map(lambda a: lax.dynamic_index_in_dim(a, source, 0, False), gathered)
        )

    return lax.fori_loop(0, ahead, one, state)


def compose(earlier, later):
    greatest_accuracy = lax.Precision.HIGHEST
    return (
        jnp.dot(later[0], earlier[0], precision=greatest_accuracy),
        jnp.dot(later[0], earlier[1], precision=greatest_accuracy) + later[1],
    )


def on_device(propagator_matrices, gain, obs_matrix, observations, present, initial, smoother_gain):
    greatest_accuracy = lax.Precision.HIGHEST
    part_rows = propagator_matrices.shape[1]
    width = propagator_matrices.shape[2]
    epochs_per_group = propagator_matrices.shape[0]
    coupling = jnp.dot(gain, obs_matrix, precision=greatest_accuracy)
    weights = present.astype(jnp.float32)
    drive = jnp.einsum("so,do->sd", observations, gain, precision=greatest_accuracy)
    full_trans, full_smooth = (
        lax.all_gather(propagator_matrices, "row", axis=1, tiled=True),
        lax.all_gather(smoother_gain, "row", axis=0, tiled=True),
    )

    def forward(state, inputs):
        matrix, forced_response, weight = inputs
        pred = jnp.dot(matrix, state, precision=greatest_accuracy)
        new_state = pred + weight * (
            forced_response - jnp.dot(coupling, pred, precision=greatest_accuracy)
        )
        return (new_state, (new_state, new_state - pred))

    def backward(carried, term):
        new_carried = jnp.dot(full_smooth, carried, precision=greatest_accuracy) + term
        return (new_carried, new_carried)

    zeros = jnp.zeros((width,), jnp.float32)
    identity = jnp.eye(width, dtype=jnp.float32)
    local_offset, _ = lax.scan(forward, zeros, (full_trans, drive, weights))
    row_start = lax.axis_index("row") * part_rows
    row_ids = lax.broadcasted_iota(jnp.int32, (part_rows, width), 0) + row_start
    col_ids = lax.broadcasted_iota(jnp.int32, (part_rows, width), 1)
    unit_matrix_lines = (row_ids == col_ids).astype(jnp.float32)

    def postmultiply_operator(carry, inputs):
        matrix, weight = inputs
        mixed = carry - weight * jnp.dot(carry, coupling, precision=greatest_accuracy)
        return (jnp.dot(mixed, matrix, precision=greatest_accuracy), None)

    map_rows, _ = lax.scan(
        postmultiply_operator, unit_matrix_lines, (full_trans, weights), reverse=True
    )
    power_rows = lax.fori_loop(
        0,
        epochs_per_group - 1,
        lambda index, acc: jnp.dot(acc, full_smooth, precision=greatest_accuracy),
        smoother_gain,
    )
    slab_map, power = (
        lax.all_gather(map_rows, "row", axis=0, tiled=True),
        lax.all_gather(power_rows, "row", axis=0, tiled=True),
    )
    prefix_map, prefix_offset = carried_in(
        (slab_map, local_offset), "slab", compose, (identity, zeros), False
    )
    start_state = jnp.dot(prefix_map, initial, precision=greatest_accuracy) + prefix_offset
    _, (filtered, correction) = lax.scan(forward, start_state, (full_trans, drive, weights))
    local_carried, _ = lax.scan(backward, zeros, correction, reverse=True)
    _, next_carried = carried_in((power, local_carried), "slab", compose, (identity, zeros), True)
    _, carried = lax.scan(backward, next_carried, correction, reverse=True)
    smoothed = filtered + carried - correction
    return (filtered, smoothed)


def solution(mesh):
    placed = (P("slab", "row", None), P(), P(), P("slab", None), P("slab"), P(), P("row", None))
    return jax.shard_map(
        on_device,
        mesh=mesh,
        in_specs=placed,
        out_specs=(P("slab", None), P("slab", None)),
        check_vma=False,
    )
```

profile of v0, /device:TPU:0, one launch (start us, length us, event | category | flops | bytes accessed | tf_op | source)
XLA Modules:
  0.0 324.6 jit_solution(9640601542221443507)
XLA Ops:
  7.2 0.7 all-gather.13.cloned.1.call-update
  8.0 0.7 all-gather.17.cloned.1.call-update
  8.7 0.7 convert_element_type.11
  9.5 1.9 fusion.34
  11.4 36.5 %all-gather.13.cloned.1.call-done = f32[2,512,512]{2,1,0:T(8,128)} async-done(((f32[2,128,512]{2,1,0:T(8,128)}), f32[2,512,512]{2,1,0:T(8,128)}) %all-gather.13.cloned.1.call-update) | async-done | bytes 2097168 | tf_op jit(solution)/shard_map/all_gather | solution.py:40
  47.9 7.8 %while.100 = (s32[]{:T(128)}, f32[128,512]{1,0:T(8,128)S(1)}, f32[2]{0:T(128)S(1)}, f32[512,512]{1,0:T(8,128)S(1)}, f32[2,512,512]{2,1,0:T(8,128)}, /*index=5*/s32[]{:T(128)}) while((s32[]{:T(128)}, f32[128,512]{1,0:T(8,128)S(1)}, f32[2]{0:T(128)S(1)}, f32[512,512]{1,0:T(8,128)S(1)}, f32[2,512,512]{2,1,0:T(8,128)}, /*index=5*/s32[]{:T(128)}) %tuple.172), condition=%wide.region_1.2_spmd, body=%wide.region_0.1_spmd.sunk | while | flops 805437440 | bytes 3145829 | solution.py:69
  48.5 1.4 fusion.98
  49.9 1.9 fusion.99
  52.4 1.4 fusion.98
  53.8 1.9 fusion.99
  55.7 0.7 copy-done.2
  56.5 19.9 %all-gather.17.cloned.1.call-done = f32[512,512]{1,0:T(8,128)} async-done(((f32[128,512]{1,0:T(8,128)}), f32[512,512]{1,0:T(8,128)}) %all-gather.17.cloned.1.call-update) | async-done | bytes 1048592 | tf_op jit(solution)/shard_map/all_gather | solution.py:41
  76.4 2.6 fusion.37
  79.1 25.8 %all-gather.15.cloned.1.call-done = f32[512,512]{1,0:T(8,128)} async-done(((f32[128,512]{1,0:T(8,128)}), f32[512,512]{1,0:T(8,128)}) %all-gather.15.cloned.1.call-update) | async-done | bytes 1048592 | tf_op jit(solution)/shard_map/all_gather | solution.py:79
  105.0 28.3 %all-gather.19.cloned.1.call-done = f32[512,512]{1,0:T(8,128)} async-done(((f32[128,512]{1,0:T(8,128)}), f32[512,512]{1,0:T(8,128)}) %all-gather.19.cloned.1.call-update) | async-done | bytes 1048592 | tf_op jit(solution)/shard_map/all_gather | solution.py:80
  133.8 9.1 %while.105 = (s32[]{:T(128)}, f32[512]{0:T(512)S(1)}, f32[2,512,512]{2,1,0:T(8,128)}, f32[2]{0:T(128)S(1)}, f32[2,512]{1,0:T(2,128)S(1)}, /*index=5*/f32[512,512]{1,0:T(8,128)S(1)}, s32[]{:T(128)}, s32[]{:T(128)}) while((s32[]{:T(128)}, f32[512]{0:T(512)S(1)}, f32[2,512,512]{2,1,0:T(8,128)}, f32[2]{0:T(128)S(1)}, ...), condition=%wide.region_3.4_spmd.clone, body=%wide.region_2.3_spmd.clone.sunk | while | flops 6293507 | bytes 2122355 | solution.py:58
  133.8 2.2 fusion.123
  136.0 1.0 fusion.124
  137.0 0.7 dynamic_slice.143
  137.6 0.7 multiply_add_fusion.4
  138.3 2.2 fusion.123
  140.6 1.0 fusion.124
  142.2 0.7 multiply_add_fusion.4
  142.9 12.9 %all-gather.4 = f32[8,1,512]{2,1,0:T(1,128)S(1)} all-gather(f32[1,1,512]{2,1,0:T(1,128)S(1)} %bitcast.205), channel_id=3, replica_groups=mesh['slab'=8,'row'=4] {'slab'}, dimensions={0}, use_global_device_ids=true | all-gather | bytes 18432 | tf_op jit(solution)/shard_map/all_gather | solution.py:11
  155.8 61.1 %all-gather.21.cloned.1.call-done = f32[4096,512]{1,0:T(8,128)} async-done(((f32[512,512]{1,0:T(8,128)}), f32[4096,512]{1,0:T(8,128)}) %all-gather.21.cloned.1.call-update) | async-done | bytes 8388624 | tf_op jit(solution)/shard_map/all_gather | solution.py:11
  216.9 0.7 copy-done.5
  217.6 1.0 fusion.36
  218.6 9.2 %while.102 = (s32[]{:T(128)}, f32[512]{0:T(512)S(1)}, f32[2,512]{1,0:T(2,128)S(1)}, f32[2,512]{1,0:T(2,128)S(1)}, f32[2,512,512]{2,1,0:T(8,128)}, /*index=5*/f32...) while((s32[]{:T(128)}, f32[512]{0:T(512)S(1)}, ...), condition=%wide.region_7.8_spmd, body=%wide.region_6.7_spmd.sunk | while | flops 6293506 | bytes 2128513 | solution.py:86
  218.7 2.2 fusion.110
  220.9 1.0 fusion.111
  223.2 2.3 fusion.110
  225.5 1.0 fusion.111
  227.9 2.1 while.106
  227.9 1.0 fusion.127
  228.9 1.0 fusion.127
  230.0 47.5 %all-gather.5 = f32[8,1,512]{2,1,0:T(1,128)S(1)} all-gather(f32[1,1,512]{2,1,0:T(1,128)S(1)} %bitcast.204), channel_id=5, replica_groups=mesh['slab'=8,'row'=4] {'slab'}, dimensions={0}, use_global_device_ids=true | all-gather | bytes 18432 | tf_op jit(solution)/shard_map/all_gather | solution.py:11
  277.5 21.7 %all-gather.23.cloned.1.call-done = f32[4096,512]{1,0:T(8,128)} async-done(((f32[512,512]{1,0:T(8,128)}), f32[4096,512]{1,0:T(8,128)}) %all-gather.23.cloned.1.call-update) | async-done | bytes 8388624 | tf_op jit(solution)/shard_map/all_gather | solution.py:11
  299.1 15.8 %while.103 = (s32[]{:T(128)}, f32[512]{0:T(512)S(1)}, s32[]{:T(128)}, f32[8,512,512]{2,1,0:T(8,128)}, f32[8,512]{1,0:T(8,128)S(1)}, /*index=5*/s32[]{:T(128)}, s32[]{:T(128)}, s32[]{:T(128)}, s32[]{:T(128)}) while((s32[]{:T(128)}, f32[512]{0:T(512)S(1)}, s32[]{:T(128)}, f32[8,512,512]{2,1,0:T(8,128)}, f32[8,512]{1,0:T(8,128)S(1)}, ...), condition=%wide.region_11.12_spmd, body=%wide.region_10.11_spmd.sunk | while | flops 3146246 | bytes 1063059 | solution.py:20
  299.1 2.2 fusion.115
  301.4 2.2 fusion.115
  303.6 2.2 fusion.115
  305.9 2.2 fusion.115
  308.2 2.2 fusion.115
  310.4 2.2 fusion.115
  312.7 2.2 fusion.115
  315.0 2.1 while.104
  315.0 1.0 fusion.118
  316.1 1.0 fusion.118
  (81 shorter events, 6.4 us)
Async XLA Ops:
  7.2 2.3 copy-start
  7.2 40.7 %all-gather.13.cloned.1.call-start = ((), (), s32[]{:S(2)}) async-start(), calls=%async_computation | async-start | bytes 2621440 | tf_op jit(solution)/shard_map/all_gather | solution.py:40
  7.9 68.5 %all-gather.17.cloned.1.call-start = ((), (), s32[]{:S(2)}) async-start(), calls=%async_computation.2 | async-start | bytes 1310720 | tf_op jit(solution)/shard_map/all_gather | solution.py:41
  8.7 96.3 %all-gather.15.cloned.1.call-start = ((), (), s32[]{:S(2)}) async-start(), calls=%async_computation.1 | async-start | bytes 1310720 | tf_op jit(solution)/shard_map/all_gather | solution.py:79
  11.4 65.0 %copy-start.3 = (f32[128,512]{1,0:T(8,128)S(1)}, f32[128,512]{1,0:T(8,128)}, u32[]{:S(2)}) copy-start(f32[128,512]{1,0:T(8,128)} %param.27) | copy-start | bytes 786436
  47.9 85.5 %copy-start.6 = (f32[2,128]{1,0:T(2,128)S(1)}, f32[2,128]{1,0:T(2,128)}, u32[]{:S(2)}) copy-start(f32[2,128]{1,0:T(2,128)} %param.24) | copy-start | bytes 3076
  55.7 0.7 copy-start.2
  56.5 76.8 %all-gather.19.cloned.1.call-start = ((), (), s32[]{:S(2)}) async-start(), calls=%async_computation.3 | async-start | bytes 1310720 | tf_op jit(solution)/shard_map/all_gather | solution.py:80
  79.1 137.9 %all-gather.21.cloned.1.call-start = ((), (), s32[]{:S(2)}) async-start(), calls=%async_computation.4 | async-start | bytes 9437184 | tf_op jit(solution)/shard_map/all_gather | solution.py:11
  104.9 194.2 %all-gather.23.cloned.1.call-start = ((), (), s32[]{:S(2)}) async-start(), calls=%async_computation.5 | async-start | bytes 9437184 | tf_op jit(solution)/shard_map/all_gather | solution.py:11
  216.9 0.7 copy-start.5
  216.9 10.9 %copy-start.1 = (f32[512,512]{1,0:T(8,128)S(1)}, f32[512,512]{1,0:T(8,128)}, u32[]{:S(2)}) copy-start(f32[512,512]{1,0:T(8,128)} %all-gather.17.cloned.1.call-done) | copy-start | bytes 3145732
  227.8 89.9 %copy-start.4 = (f32[2,512]{1,0:T(2,128)}, f32[2,512]{1,0:T(2,128)S(1)}, u32[]{:S(2)}) copy-start(f32[2,512]{1,0:T(2,128)S(1)} %get-tuple-element.492) | copy-start | bytes 12292
Sparse Core Ops, SparseCore 0:
  9.9 38.0 all-gather.12
  49.7 26.6 all-gather.16
  78.3 26.6 all-gather.14
  106.6 26.6 all-gather.18
  134.7 82.1 all-gather.20
  218.4 80.6 all-gather.22
where the time goes:
time: 326 us; the launch traced here: 325 us
  waiting for transfers between devices  195 us (60%)
  blocking collectives  60.4 us (19%)
  matrix products  44.6 us (14%)
  between operations  14.3 us (4%)
  local copies, waits for them, and re-layouts  5.58 us (2%)
  other arithmetic  4.22 us (1%)
    all_gather x2, waiting for transfers between devices, carried_in(): gathered = jax.tree.map(lambda a: lax.all_gather(a, axis), part)  82.7 us
    all_gather x2, blocking collectives, carried_in(): gathered = jax.tree.map(lambda a: lax.all_gather(a, axis), part)  60.4 us
    all_gather x1, waiting for transfers between devices, on_device(): lax.all_gather(propagator_matrices, 'row', axis=1, tiled=True)  36.5 us
    all_gather x1, waiting for transfers between devices, on_device(): lax.all_gather(power_rows, 'row', axis=0, tiled=True)  28.3 us
    all_gather x1, waiting for transfers between devices, on_device(): lax.all_gather(map_rows, 'row', axis=0, tiled=True)  25.8 us
    all_gather x1, waiting for transfers between devices, on_device(): lax.all_gather(smoother_gain, 'row', axis=0, tiled=True)  19.9 us
    dot_general x7, matrix products, compose(): jnp.dot(later[0], earlier[1], precision=greatest_accuracy) + later[1]  15.4 us
    dot_general x4, matrix products, forward(): pred = jnp.dot(matrix, state, precision=greatest_accuracy)  8.93 us
  transfers between devices with their start and end apart: 6, of which 6 were waited for; matrix products, arithmetic and copies ran while one was open for 11% of the time, Pallas kernels for 0%

commit v1 on v0

--- a/solution.py
+++ b/solution.py
@@ -2,6 +2,29 @@
 import jax.numpy as jnp
 from jax import lax
 from jax.sharding import PartitionSpec as P
+
+
+def state_object(base_x):
+    before, newest, tall = (lax.axis_size("row"), lax.axis_index("row"), base_x.shape[1])
+    crops = []
+    for i in range(before):
+        crops.append((i, (i + 1) % before))
+    seen = []
+    for i in range(before):
+        seen.append((i, (i - 1) % before))
+    y2 = jnp.zeros((*base_x.shape[:1], before * tall, *base_x.shape[2:]), base_x.dtype)
+    y2 = lax.dynamic_update_slice_in_dim(y2, base_x, newest * tall, axis=1)
+    out_arr = kept_arr = base_x
+    step_out = before // 2
+    for ix in range(1, step_out + 1):
+        out_arr = lax.ppermute(out_arr, axis_name="row", perm=crops)
+        y2 = lax.dynamic_update_slice_in_dim(y2, out_arr, (newest - ix) % before * tall, axis=1)
+        if ix < before - step_out:
+            kept_arr = lax.ppermute(kept_arr, axis_name="row", perm=seen)
+            y2 = lax.dynamic_update_slice_in_dim(
+                y2, kept_arr, (newest + ix) % before * tall, axis=1
+            )
+    return y2
 
 
 def carried_in(part, axis, combine, identity, reverse):
@@ -37,7 +60,7 @@
     weights = present.astype(jnp.float32)
     drive = jnp.einsum("so,do->sd", observations, gain, precision=greatest_accuracy)
     full_trans, full_smooth = (
-        lax.all_gather(propagator_matrices, "row", axis=1, tiled=True),
+        state_object(propagator_matrices),
         lax.all_gather(smoother_gain, "row", axis=0, tiled=True),
     )
 

time: 326 us -> 313 us (0.960)
  waiting for transfers between devices: 195 us -> 157 us
  blocking collectives: 60.4 us -> 75.2 us
  starting transfers between devices: 0.23 us -> 6.69 us
    all_gather x1 -> x0, waiting for transfers between devices: 36.5 us -> none  [on_device(): lax.all_gather(propagator_matrices, 'row', axis=1, tiled=True)]
    ppermute x0 -> x3, waiting for transfers between devices: none -> 35.2 us  [the longest x2 23.2 us: state_object(): out_arr = lax.ppermute(out_arr, axis_name='row', perm=crops)]
    all_gather x1, waiting for transfers between devices: 19.9 us -> 0.02 us  [on_device(): lax.all_gather(smoother_gain, 'row', axis=0, tiled=True)]
    all_gather x2, blocking collectives: 60.4 us -> 75.2 us  [carried_in(): gathered = jax.tree.map(lambda a: lax.all_gather(a, axis), part)]
    all_gather x2, waiting for transfers between devices: 82.7 us -> 68.4 us  [carried_in(): gathered = jax.tree.map(lambda a: lax.all_gather(a, axis), part)]
    ppermute x0 -> x3, starting transfers between devices: none -> 6.49 us  [the longest x2 5.47 us: state_object(): out_arr = lax.ppermute(out_arr, axis_name='row', perm=crops)]
    dot_general x4, matrix products: 8.93 us -> 3.97 us  [forward(): pred = jnp.dot(matrix, state, precision=greatest_accuracy)]
    dynamic_update_slice x0 -> x4, local copies, waits for them, and re-layouts: none -> 3.28 us  [the longest x2 2.15 us: state_object(): lax.dynamic_update_slice_in_dim(y2, out_arr, (newest - ix) % before * tal...]
  transfers between devices with their start and end apart: 6 -> 8, of which waited for: 6 -> 7; matrix products, arithmetic and copies ran while one was open for 11% -> 13% of each run, Pallas kernels for 0% -> 0%
where the time goes in v1:
time: 313 us; the launch traced here: 311 us
  waiting for transfers between devices  157 us (50%)
  blocking collectives  75.2 us (24%)
  matrix products  44.7 us (14%)
  between operations  14 us (4%)
  local copies, waits for them, and re-layouts  8.33 us (3%)
  starting transfers between devices  6.69 us (2%)
  other arithmetic  5.2 us (2%)
    all_gather x2, blocking collectives, carried_in(): gathered = jax.tree.map(lambda a: lax.all_gather(a, axis), part)  75.2 us
    all_gather x2, waiting for transfers between devices, carried_in(): gathered = jax.tree.map(lambda a: lax.all_gather(a, axis), part)  68.4 us
    all_gather x1, waiting for transfers between devices, on_device(): lax.all_gather(power_rows, 'row', axis=0, tiled=True)  28.4 us
    all_gather x1, waiting for transfers between devices, on_device(): lax.all_gather(map_rows, 'row', axis=0, tiled=True)  24.5 us
    ppermute x2, waiting for transfers between devices, state_object(): out_arr = lax.ppermute(out_arr, axis_name='row', perm=crops)  23.2 us
    dot_general x7, matrix products, compose(): jnp.dot(later[0], earlier[1], precision=greatest_accuracy) + later[1]  15.5 us
    ppermute x1, waiting for transfers between devices, state_object(): kept_arr = lax.ppermute(kept_arr, axis_name='row', perm=seen)  12 us
    dot_general x4, matrix products, backward(): jnp.dot(full_smooth, carried, precision=greatest_accuracy) + term  6.45 us
  transfers between devices with their start and end apart: 8, of which 7 were waited for; matrix products, arithmetic and copies ran while one was open for 13% of the time, Pallas kernels for 0%

profile of v1, /device:TPU:0, one launch (start us, length us, event | category | flops | bytes accessed | tf_op | source)
XLA Modules:
  0.0 311.3 jit_solution(8508995134935546654)
XLA Ops:
  7.2 3.0 collective-permute-start
  10.2 1.0 collective-permute-start.1
  11.3 2.0 fusion.34
  13.7 11.3 %collective-permute-done = f32[2,128,512]{2,1,0:T(8,128)} collective-permute-done((f32[2,128,512]{2,1,0:T(8,128)}, f32[2,128,512]{2,1,0:T(8,128)}, u32[]{:S(2)}, u32[]{:S(2)}) %collective-permute-start) | collective-permute-done | bytes 524320 | tf_op jit(solution)/shard_map/ppermute | solution.py:20
  25.0 2.5 collective-permute-start.2
  28.3 1.1 constant_dynamic-update-slice_fusion.2
  29.4 12.0 %collective-permute-done.1 = f32[2,128,512]{2,1,0:T(8,128)} collective-permute-done((f32[2,128,512]{2,1,0:T(8,128)}, f32[2,128,512]{2,1,0:T(8,128)}, u32[]{:S(2)}, u32[]{:S(2)}) %collective-permute-start.1) | collective-permute-done | bytes 524320 | tf_op jit(solution)/shard_map/ppermute | solution.py:23
  41.4 1.1 constant_dynamic-update-slice_fusion.1
  42.5 11.8 %collective-permute-done.2 = f32[2,128,512]{2,1,0:T(8,128)} collective-permute-done((f32[2,128,512]{2,1,0:T(8,128)}, f32[2,128,512]{2,1,0:T(8,128)}, u32[]{:S(2)}, u32[]{:S(2)}) %collective-permute-start.2) | collective-permute-done | bytes 524320 | tf_op jit(solution)/shard_map/ppermute | solution.py:20
  54.3 1.1 constant_dynamic-update-slice_fusion
  55.4 8.9 %while.100 = (s32[]{:T(128)}, f32[128,512]{1,0:T(8,128)}, f32[2]{0:T(128)S(1)}, f32[512,512]{1,0:T(8,128)S(1)}, f32[2,512,512]{2,1,0:T(8,128)S(1)}, /*index=5*/s32[]{:T(128)}) while((s32[]{:T(128)}, f32[128,512]{1,0:T(8,128)}, f32[2]{0:T(128)S(1)}, f32[512,512]{1,0:T(8,128)S(1)}, f32[2,512,512]{2,1,0:T(8,128)S(1)}, /*index=5*/s32[]{:T(128)}) %tuple.172), condition=%wide.region_1.2_spmd, body=%wide.region_0.1_spmd.sunk | while | flops 805437440 | bytes 3145829 | solution.py:92
  56.0 2.4 fusion.98
  58.4 1.5 fusion.99
  60.4 2.4 fusion.98
  62.8 1.5 fusion.99
  64.4 2.7 fusion.37
  67.2 24.5 %all-gather.12.cloned.1.call-done = f32[512,512]{1,0:T(8,128)} async-done(((f32[128,512]{1,0:T(8,128)}), f32[512,512]{1,0:T(8,128)}) %all-gather.12.cloned.1.call-update) | async-done | bytes 1048592 | tf_op jit(solution)/shard_map/all_gather | solution.py:102
  91.7 28.4 %all-gather.16.cloned.1.call-done = f32[512,512]{1,0:T(8,128)} async-done(((f32[128,512]{1,0:T(8,128)}), f32[512,512]{1,0:T(8,128)}) %all-gather.16.cloned.1.call-update) | async-done | bytes 1048592 | tf_op jit(solution)/shard_map/all_gather | solution.py:103
  120.2 1.1 fusion.29
  121.6 6.5 %while.105 = (s32[]{:T(128)}, f32[512]{0:T(512)S(1)}, f32[2,512,512]{2,1,0:T(8,128)S(1)}, f32[2]{0:T(128)S(1)}, f32[2,512]{1,0:T(2,128)S(1)}, /*index=5*/f32[512,512]{1,0:T(8,128)S(1)}, s32[]{:T(128)}, s32[]{:T(128)}) while((s32[]{:T(128)}, f32[512]{0:T(512)S(1)}, f32[2,512,512]{2,1,0:T(8,128)S(1)}, f32[2]{0:T(128)S(1)}, ...), condition=%wide.region_3.4_spmd.clone, body=%wide.region_2.3_spmd.clone.sunk | while | flops 6293507 | bytes 2121847 | solution.py:81
  121.6 1.0 fusion.123
  122.6 1.0 fusion.124
  124.9 1.0 fusion.123
  125.9 1.0 fusion.124
  128.1 13.2 %all-gather.4 = f32[8,1,512]{2,1,0:T(1,128)S(1)} all-gather(f32[1,1,512]{2,1,0:T(1,128)S(1)} %bitcast.205), channel_id=3, replica_groups=mesh['slab'=8,'row'=4] {'slab'}, dimensions={0}, use_global_device_ids=true | all-gather | bytes 18432 | tf_op jit(solution)/shard_map/all_gather | solution.py:34
  141.4 62.5 %all-gather.18.cloned.1.call-done = f32[4096,512]{1,0:T(8,128)} async-done(((f32[512,512]{1,0:T(8,128)}), f32[4096,512]{1,0:T(8,128)}) %all-gather.18.cloned.1.call-update) | async-done | bytes 8388624 | tf_op jit(solution)/shard_map/all_gather | solution.py:34
  204.5 2.2 fusion.36
  206.8 6.7 %while.102 = (s32[]{:T(128)}, f32[512]{0:T(512)S(1)}, f32[2,512]{1,0:T(2,128)S(1)}, f32[2,512]{1,0:T(2,128)S(1)}, f32[2,512,512]{2,1,0:T(8,128)S(1)}, /*index=5*...) while((s32[]{:T(128)}, f32[512]{0:T(512)S(1)}, ...), condition=%wide.region_7.8_spmd, body=%wide.region_6.7_spmd.sunk | while | flops 6293506 | bytes 2128005 | solution.py:109
  206.8 1.0 fusion.110
  207.8 1.0 fusion.111
  210.1 1.0 fusion.110
  211.1 1.0 fusion.111
  213.5 4.6 %while.106 = (s32[]{:T(128)}, f32[512]{0:T(512)S(1)}, f32[512,512]{1,0:T(8,128)}, f32[2,512]{1,0:T(2,128)S(1)}, s32[]{:T(128)}, /*index=5*/s32[]{:T(128)}) while((s32[]{:T(128)}, f32[512]{0:T(512)S(1)}, f32[512,512]{1,0:T(8,128)}, f32[2,512]{1,0:T(2,128)S(1)}, s32[]{:T(128)}, /*index=5*/s32[]{:T(128)}) %tuple.184), condition=%wide.region_9.10_spmd.clone, body=%wide.region_8.9_spmd.clone.sunk | while | flops 3146756 | bytes 1067103 | solution.py:110
  213.5 2.3 fusion.127
  215.9 2.2 fusion.127
  218.1 62.0 %all-gather.5 = f32[8,1,512]{2,1,0:T(1,128)S(1)} all-gather(f32[1,1,512]{2,1,0:T(1,128)S(1)} %bitcast.204), channel_id=5, replica_groups=mesh['slab'=8,'row'=4] {'slab'}, dimensions={0}, use_global_device_ids=true | all-gather | bytes 18432 | tf_op jit(solution)/shard_map/all_gather | solution.py:34
  280.1 5.9 %all-gather.20.cloned.1.call-done = f32[4096,512]{1,0:T(8,128)} async-done(((f32[512,512]{1,0:T(8,128)}), f32[4096,512]{1,0:T(8,128)}) %all-gather.20.cloned.1.call-update) | async-done | bytes 8388624 | tf_op jit(solution)/shard_map/all_gather | solution.py:34
  286.0 15.9 %while.103 = (s32[]{:T(128)}, f32[512]{0:T(512)S(1)}, s32[]{:T(128)}, f32[8,512,512]{2,1,0:T(8,128)}, f32[8,512]{1,0:T(8,128)S(1)}, /*index=5*/s32[]{:T(128)}, s32[]{:T(128)}, s32[]{:T(128)}, s32[]{:T(128)}) while((s32[]{:T(128)}, f32[512]{0:T(512)S(1)}, s32[]{:T(128)}, f32[8,512,512]{2,1,0:T(8,128)}, f32[8,512]{1,0:T(8,128)S(1)}, ...), condition=%wide.region_11.12_spmd, body=%wide.region_10.11_spmd.sunk | while | flops 3146246 | bytes 1063059 | solution.py:43
  286.0 2.3 fusion.115
  288.4 2.2 fusion.115
  290.6 2.2 fusion.115
  292.9 2.2 fusion.115
  295.2 2.2 fusion.115
  297.4 2.2 fusion.115
  299.7 2.2 fusion.115
  302.0 2.1 while.104
  302.0 1.0 fusion.118
  303.1 1.0 fusion.118
  (89 shorter events, 9.8 us)
Async XLA Ops:
  7.2 4.2 %copy-start = (f32[512,128]{1,0:T(8,128)S(1)}, f32[512,128]{1,0:T(8,128)}, u32[]{:S(2)}) copy-start(f32[512,128]{1,0:T(8,128)} %param.22) | copy-start | bytes 786436
  7.2 57.2 %all-gather.14.cloned.1.call-start = ((), (), s32[]{:S(2)}) async-start(), calls=%async_computation.1 | async-start | bytes 1310720 | tf_op jit(solution)/shard_map/all_gather | solution.py:64
  7.2 17.8 %collective-permute-start = (f32[2,128,512]{2,1,0:T(8,128)}, f32[2,128,512]{2,1,0:T(8,128)}, u32[]{:S(2)}, u32[]{:S(2)}) collective-permute-start(f32[2,128,512]{2,1,0:T(8,128)} %param.21), channel_id=1, source_target_pairs={{0,1},{1,2},{2,3},{3,0},{4,5},{5,6},{6,7},{7,4},{8,9},{9,10},{10,1... | collective-permute-start | bytes 1572872 | tf_op jit(solution)/shard_map/ppermute | solution.py:20
  10.2 31.2 %collective-permute-start.1 = (f32[2,128,512]{2,1,0:T(8,128)}, f32[2,128,512]{2,1,0:T(8,128)}, u32[]{:S(2)}, u32[]{:S(2)}) collective-permute-start(f32[2,128,512]{2,1,0:T(8,128)} %param.21), channel_id=1, source_target_pairs={{0,3},{1,0},{2,1},{3,2},{4,7},{5,4},{6,5},{7,6},{8,11},{9,8},{10,9... | collective-permute-start | bytes 1572872 | tf_op jit(solution)/shard_map/ppermute | solution.py:23
  11.3 80.4 %all-gather.12.cloned.1.call-start = ((), (), s32[]{:S(2)}) async-start(), calls=%async_computation | async-start | bytes 1310720 | tf_op jit(solution)/shard_map/all_gather | solution.py:102
  11.3 2.3 copy-start.2
  11.3 16.1 %copy-start.6 = (s32[2]{0:T(128)S(1)}, s32[2]{0:T(128)}, u32[]{:S(2)}) copy-start(s32[2]{0:T(128)} %param.25) | copy-start | bytes 28
  25.0 29.3 %collective-permute-start.2 = (f32[2,128,512]{2,1,0:T(8,128)}, f32[2,128,512]{2,1,0:T(8,128)}, u32[]{:S(2)}, u32[]{:S(2)}) collective-permute-start(f32[2,128,512]{2,1,0:T(8,128)} %collective-permute-done), channel_id=1, source_target_pairs={{0,1},{1,2},{2,3},{3,0},{4,5},{5,6},{6,7},{7,4},{8,9},{9,10},{10,1... | collective-permute-start | bytes 1572872 | tf_op jit(solution)/shard_map/ppermute | solution.py:20
  64.3 55.8 %all-gather.16.cloned.1.call-start = ((), (), s32[]{:S(2)}) async-start(), calls=%async_computation.2 | async-start | bytes 1310720 | tf_op jit(solution)/shard_map/all_gather | solution.py:103
  67.1 54.2 %copy-start.5 = (f32[2,128]{1,0:T(2,128)S(1)}, f32[2,128]{1,0:T(2,128)}, u32[]{:S(2)}) copy-start(f32[2,128]{1,0:T(2,128)} %param.24) | copy-start | bytes 3076
  67.2 136.7 %all-gather.18.cloned.1.call-start = ((), (), s32[]{:S(2)}) async-start(), calls=%async_computation.3 | async-start | bytes 9437184 | tf_op jit(solution)/shard_map/all_gather | solution.py:34
  91.7 194.3 %all-gather.20.cloned.1.call-start = ((), (), s32[]{:S(2)}) async-start(), calls=%async_computation.4 | async-start | bytes 9437184 | tf_op jit(solution)/shard_map/all_gather | solution.py:34
  203.9 0.7 copy-start.4
  213.5 90.7 %copy-start.3 = (f32[2,512]{1,0:T(2,128)}, f32[2,512]{1,0:T(2,128)S(1)}, u32[]{:S(2)}) copy-start(f32[2,512]{1,0:T(2,128)S(1)} %get-tuple-element.492) | copy-start | bytes 12292
  286.0 16.0 %copy-start.1 = (f32[512,512]{1,0:T(8,128)S(1)}, f32[512,512]{1,0:T(8,128)}, u32[]{:S(2)}) copy-start(f32[512,512]{1,0:T(8,128)} %get-tuple-element.1041) | copy-start | bytes 3145732
Sparse Core Ops, SparseCore 0:
  11.4 36.3 all-gather.13
  64.4 27.1 all-gather.11
  93.5 26.6 all-gather.15
  121.6 82.2 all-gather.17
  205.3 80.6 all-gather.19
